TPU v7x, 256 devices: a whole 4x4x8 slice. The times are simulated.
256 devices in a mesh: row: 16 (over y_hi, z), col: 16 (over x, y_lo, core).
Axes of the slice: x: 4, y: 4 (y_hi: 2, y_lo: 2; y = y_hi * 2 + y_lo), z: 8, core: 2. Of those that a mesh axis runs over, the one named last changes fastest.
Arguments:
- amplitudes: bfloat16 [49152, 12288], P('row', 'col'), may hold values from -6 to 6
- pair_mask: int32 [192, 48], P('row', 'col'), may hold values 0 or 1
- integrals: bfloat16 [16, 16, 2, 256, 256], P('row', 'col'), may hold values from -0.25 to 0.25
- tile_list: int32 [16, 16, 2], P('row', 'col'), may hold values from 0 to 2, as said below
- tile_count: int32 [16, 16], P('row', 'col'), may hold values from 1 to 2, as said below
- owner: int32 [4, 16], P(None, 'col'), may hold values from 0 to 15, as said below
Outputs:
- ladder: bfloat16 [49152, 4096], P('row', 'col')
Inputs may be any that keep to these rules, and one draw needn't show every extreme that they name: `owner`: within a column the 4 owners differ. `tile_count`: some panel that serves a step has all 2 slots live. `tile_list`: the live slots of a panel name distinct cd tile pairs; entries past the count are in range and unused.
All inputs are finite; a program needn't handle non-finite values. No bound on the sum of `pair_mask` on one device may be relied on, other than what follows from the above.
Results may differ from a plain program's by a relative error of at most 0.001.
Values may be sent and summed in bfloat16 or wider, within the bound.
A program may use at most 128 MiB of HBM per device.

v0:
```python
import jax
import jax.numpy as jnp
from jax import lax
from jax.sharding import PartitionSpec as P

STEPS = 4


def passed_along(value, axis, by):
    peers = lax.axis_size(axis)
    return lax.ppermute(value, axis, [(i, (i + by) % peers) for i in range(peers)])


def broadcast(value, axis, source):
    kept = jnp.where(lax.axis_index(axis) == source, value, 0).astype(value.dtype)
    return lax.psum(kept, axis)


def slot_product(current, panel_tiles, slot_tiles, slot_index, tile_width):
    start = slot_tiles[slot_index] * tile_width
    tile_block = lax.dynamic_slice_in_dim(current, start, tile_width, 1)
    weights = lax.dynamic_index_in_dim(panel_tiles, slot_index, 0, keepdims=False)
    return jnp.dot(tile_block, weights, preferred_element_type=jnp.float32)


def shards(amplitudes, pair_mask, integrals, tile_list, tile_count, owner):
    row_count, full_width = amplitudes.shape
    tile_width = integrals.shape[-1]
    block_count, local_tiles = pair_mask.shape
    slot_total = integrals.shape[2]
    shaped = amplitudes.reshape(block_count, row_count // block_count, local_tiles, tile_width)
    masked = (shaped * pair_mask.astype(jnp.bfloat16)[:, None, :, None]).reshape(
        row_count, full_width
    )
    running = jnp.zeros((row_count, tile_width), jnp.float32)
    current = masked
    for grid_step in range(STEPS):
        if grid_step > 0:
            current = passed_along(current, "col", 1)
        panel_tiles, slot_tiles, live_count = (
            broadcast(integrals[0, 0], "row", owner[grid_step, 0]),
            broadcast(tile_list[0, 0], "row", owner[grid_step, 0]),
            broadcast(tile_count[0, 0], "row", owner[grid_step, 0]),
        )
        for slot_index in range(slot_total):
            product = slot_product(current, panel_tiles, slot_tiles, slot_index, tile_width)
            running = running + jnp.where(slot_index < live_count, product, jnp.zeros_like(product))
    return running.astype(jnp.bfloat16)


def solution(mesh):
    return jax.shard_map(
        shards,
        mesh=mesh,
        in_specs=(
            P("row", "col"),
            P("row", "col"),
            P("row", "col", None, None, None),
            P("row", "col", None),
            P("row", "col"),
            P(None, "col"),
        ),
        out_specs=P("row", "col"),
        check_vma=False,
    )
```

profile of v0, /device:TPU:2, one launch (start us, length us, event | category | flops | bytes accessed | tf_op | source)
XLA Modules:
  0.0 333.6 jit_solution(6793563908620637323)
XLA Ops:
  6.5 0.7 convert_element_type.11
  7.2 0.5 mul.59
  7.7 5.3 %copy.9 = bf16[96,8,12,256]{3,1,2,0:T(8,128)(2,1)} copy(bf16[96,8,12,256]{3,2,1,0:T(8,128)(2,1)S(1)} %bitcast.62) | data formatting | bytes 9437184
  13.0 6.6 %copy.8 = bf16[3072,768]{0,1:T(8,128)(2,1)} copy(bf16[3072,768]{1,0:T(8,128)(2,1)} %param.6) | data formatting | bytes 9437184 | tf_op args[0]
  19.7 5.7 %mul.61 = bf16[3072,768]{0,1:T(8,128)(2,1)S(1)} multiply(bf16[3072,768]{0,1:T(8,128)(2,1)} %copy.8, bf16[3072,768]{0,1:T(8,128)(2,1)} %bitcast.63) | non-fusion elementwise | flops 2359296 | bytes 14155776 | tf_op jit(solution)/shard_map/mul | solution.py:32
  25.4 2.1 copy-done
  27.5 0.0 collective-permute-start
  27.5 54.4 %collective-permute-done = bf16[3072,768]{0,1:T(8,128)(2,1)S(1)} collective-permute-done((bf16[3072,768]{0,1:T(8,128)(2,1)S(1)}, bf16[3072,768]{0,1:T(8,128)(2,1)S(1)}, u32[]{:S(2)}, u32[]{:S(2)}) %collective-permute-start) | collective-permute-done | bytes 4718624 | tf_op jit(solution)/shard_map/ppermute | solution.py:11
  82.0 2.2 copy-done.1
  84.2 0.0 collective-permute-start.1
  84.2 54.5 %collective-permute-done.1 = bf16[3072,768]{0,1:T(8,128)(2,1)} collective-permute-done((bf16[3072,768]{0,1:T(8,128)(2,1)S(1)}, bf16[3072,768]{0,1:T(8,128)(2,1)}, u32[]{:S(2)}, u32[]{:S(2)}) %collective-permute-start.1) | collective-permute-done | bytes 4718624 | tf_op jit(solution)/shard_map/ppermute | solution.py:11
  138.8 0.0 collective-permute-start.2
  138.8 0.0 copy-done.7
  138.8 0.7 fusion.32
  142.1 1.0 select_bitcast_fusion.3
  143.0 0.0 all-reduce.4.cloned.1.call-update
  143.8 21.6 %all-reduce = (s32[2]{0:T(128)S(1)}, s32[]{:T(128)}, s32[2]{0:T(128)S(1)}, s32[]{:T(128)}, s32[2]{0:T(128)S(1)}, /*index=5*/s32[]{:T(128)}, s32[2]{0:T(128)S(1)}, s32[]{:T(128)}) all-reduce(s32[2]{0:T(128)S(1)} %get-tuple-element.31, s32[]{:T(128)S(6)} %select_n.211, ...), channel_id=1, replica_groups=mesh['row'=16,'col'=16] {'row'}, use_global_device_ids=true, to_apply=%region_10.11 | all-reduce | flops 12 | bytes 96 | tf_op jit(solution)/shard_map/psum | solution.py:16
  165.3 0.7 fusion.30
  171.1 0.7 fusion.28
  176.9 134.2 %all-reduce.4.cloned.1.call-done = (bf16[2,256,256]{2,1,0:T(8,128)(2,1)}, bf16[2,256,256]{2,1,0:T(8,128)(2,1)}, bf16[2,256,256]{2,1,0:T(8,128)(2,1)}, bf16[2,256,256]{2,1,0:T(8,128)(2,1)}) async-done(((bf16[2,256,256]{2,1,0:T(8,128)(2,1)}, bf16[2,256,256]{2,1,0:T(8,128)(2,1)}, bf16[2,256,256]{2,1,0:T(8,128)(2,1)}, bf16[2,256,256]{2,1,0:T(8,128)(2,1)}), (bf16[2,256,256]{2,1,0:T(8,128)(2,1)}, ...) | async-done | bytes 1048592 | tf_op jit(solution)/shard_map/psum | solution.py:16
  311.1 2.2 convolution_select_fusion.6
  313.3 0.0 slice-start.1
  313.3 2.2 fusion
  315.5 0.0 slice-done
  315.5 0.6 convolution_select_fusion.4
  316.1 0.7 fusion.2
  316.8 0.3 copy-done.4
  317.1 2.0 convolution_select_fusion.2
  319.1 2.2 fusion.4
  321.3 0.0 collective-permute-done.2
  321.4 2.0 convolution_select_fusion
  323.4 3.4 %fusion.7 = bf16[3072,256]{1,0:T(8,128)(2,1)} fusion(f32[3072,256]{1,0:T(8,128)S(1)} %convolution_select_fusion, f32[3072,256]{1,0:T(8,128)S(1)} %fusion.4, bf16[3072,768]{0,1:T(8,128)(2,1)} %collective-permute-done.2, s32[]{:T(128)S(6)} %select_n.216, pred[]{:T(512)S(6)} %gt.30, bf16[2,256,256]{2,1,0:T(8,128)(2,1)S(1)} %copy-done.3), kind=kOutput, calls=%fused_computation.15 | convolution fusion | flops 405798912 | bytes 9568261 | tf_op jit(solution)/shard_map/dot_general | solution.py:23
  (19 shorter events, 0.0 us)
Async XLA Ops:
  6.5 304.5 %all-reduce.4.cloned.1.call-start = ((), (), s32[]{:S(2)}) async-start(), calls=%async_computation | async-start | bytes 2097152 | tf_op jit(solution)/shard_map/psum | solution.py:16
  19.7 119.1 %copy-start.7 = (s32[4,1]{0,1:T(1,128)S(1)}, s32[4,1]{0,1:T(1,128)}, u32[]{:S(2)}) copy-start(s32[4,1]{0,1:T(1,128)} %param.11) | copy-start | bytes 52
  19.7 122.4 %copy-start.2 = (bf16[1,1,2,256,256]{4,3,2,1,0:T(8,128)(2,1)S(1)}, bf16[1,1,2,256,256]{4,3,2,1,0:T(8,128)(2,1)}, u32[]{:S(2)}) copy-start(bf16[1,1,2,256,256]{4,3,2,1,0:T(8,128)(2,1)} %param.8) | copy-start | bytes 786436
  19.7 124.1 %copy-start.8 = (s32[1,1,2]{2,1,0:T(1,128)S(1)}, s32[1,1,2]{2,1,0:T(1,128)}, u32[]{:S(2)}) copy-start(s32[1,1,2]{2,1,0:T(1,128)} %param.9) | copy-start | bytes 28
  25.4 2.1 copy-start
  27.5 54.4 %collective-permute-start = (bf16[3072,768]{0,1:T(8,128)(2,1)S(1)}, bf16[3072,768]{0,1:T(8,128)(2,1)S(1)}, u32[]{:S(2)}, u32[]{:S(2)}) collective-permute-start(bf16[3072,768]{0,1:T(8,128)(2,1)S(1)} %mul.61), channel_id=1, source_target_pairs={{0,1},{1,2},{2,3},{3,4},{4,5},{5,6},{6,7},{7,8},{8,9},{9,10},{10,1... | collective-permute-start | bytes 14155784 | tf_op jit(solution)/shard_map/ppermute | solution.py:11
  82.0 2.2 copy-start.1
  84.2 54.6 %collective-permute-start.1 = (bf16[3072,768]{0,1:T(8,128)(2,1)S(1)}, bf16[3072,768]{0,1:T(8,128)(2,1)}, u32[]{:S(2)}, u32[]{:S(2)}) collective-permute-start(bf16[3072,768]{0,1:T(8,128)(2,1)S(1)} %collective-permute-done), channel_id=1, source_target_pairs={{0,1},{1,2},{2,3},{3,4},{4,5},{5,6},{6,7},{7,8},{8,9},{9,10},{10,1... | collective-permute-start | bytes 14155784 | tf_op jit(solution)/shard_map/ppermute | solution.py:11
  138.8 182.6 %collective-permute-start.2 = (bf16[3072,768]{0,1:T(8,128)(2,1)}, bf16[3072,768]{0,1:T(8,128)(2,1)}, u32[]{:S(2)}, u32[]{:S(2)}) collective-permute-start(bf16[3072,768]{0,1:T(8,128)(2,1)} %collective-permute-done.1), channel_id=1, source_target_pairs={{0,1},{1,2},{2,3},{3,4},{4,5},{5,6},{6,7},{7,8},{8,9},{9,10},{10,1... | collective-permute-start | bytes 14155784 | tf_op jit(solution)/shard_map/ppermute | solution.py:11
  311.1 2.2 copy-start.6
  311.1 4.4 %slice-start = ((s8[4718592]{0:T(1024)(128)(4,1)}), s8[4194304]{0:T(1024)(128)(4,1)S(1)}, s32[]{:S(2)}) async-start(s8[4718592]{0:T(1024)(128)(4,1)} %bitcast.64), calls=%async_computation.1 | async-start | bytes 8388608
  313.3 2.2 slice-start.1
  313.3 2.2 copy-start.5
  316.1 1.0 copy-start.4
  319.1 2.2 copy-start.3
Sparse Core Ops, SparseCore 0:
  143.2 167.8 all-reduce.3
where the time goes:
time: 334 us
  waiting for transfers between devices  243 us (73%)
  between operations  27.1 us (8%)
  blocking collectives  21.6 us (6%)
  local copies, waits for them, and re-layouts  19.1 us (6%)
  matrix products  15.3 us (5%)
  other arithmetic  7.4 us (2%)
    psum x1, waiting for transfers between devices, broadcast(): return lax.psum(kept, axis)  134 us
    ppermute x3, waiting for transfers between devices, passed_along(): lax.ppermute(value, axis, [(i, (i + by) % peers) for i in range(peers)])  109 us
    psum x1, blocking collectives, broadcast(): return lax.psum(kept, axis)  21.6 us
    unnamed x24, local copies, waits for them, and re-layouts  16.6 us
    dot_general x8, matrix products, slot_product(): return jnp.dot(tile_block, weights, preferred_element_type=jnp.float32)  15.3 us
  transfers between devices with their start and end apart: 4, of which 3 were waited for; matrix products, arithmetic and copies ran while one was open for 4% of the time, Pallas kernels for 0%

commit v1 on v0

v1 whole, which is shorter than its diff:
```python
import functools

import jax
import jax.numpy as jnp
from jax import lax
from jax.experimental import pallas as pl
from jax.experimental.pallas import tpu as pltpu
from jax.sharding import PartitionSpec as P

MESH = pl.DeviceIdType.MESH
F32 = jnp.float32
BF16 = jnp.bfloat16
LINK = jnp.int16
TOP = 32767.0
TINY = 1e-33


def kernel(
    rows_of, cols_of, owner_ref, list_ref, count_ref, mask_ref, amp, panel, out,
    both, maskv, meta, meta_in, piece_in, fac_out, fac_a, fac_b, q_out, p_a, p_b,
    w_a, w_b, local, t_own, s_out, s_scale, r_one, r_one_scale, t_out, t_scale, r_two, r_two_scale, result,
    amp_sem, amp_send, amp_recv, a2a_send, a2a_recv, shift_send, shift_recv,
    ring_send_a, ring_recv_a, ring_send_b, ring_recv_b, one_send, one_recv, two_send, two_recv, out_sem,
):
    r, c = lax.axis_index("row"), lax.axis_index("col")
    depth_z = rows_of // 2
    chips = cols_of // 2
    y, z = r // depth_z, r % depth_z
    chip, core = c // 2, c % 2
    y_lo = chip % 2
    tile = panel.shape[-1]
    strip = tile // rows_of
    blocks, tiles = mask_ref.shape
    block = amp.shape[0] // blocks
    width = amp.shape[1]

    def at_chip(step, same_core=True):
        return lax.rem(chip + step + chips, chips) * 2 + core

    row_id = lax.broadcasted_iota(jnp.int32, (8, 128), 0)
    flags = jnp.zeros((8, 128), F32)
    for k in range(2):
        live = jnp.where(k < count_ref[0, 0], k * tiles + list_ref[0, 0, k], -1)
        flags = flags + jnp.where(row_id == live, 1.0, 0.0)
    meta[...] = flags
    meta_in[r] = flags
    for b in range(blocks):
        for t in range(tiles):
            maskv[core, b : b + 1, t * tile : (t + 1) * tile] = jnp.full(
                (1, tile), mask_ref[b, t].astype(F32), F32
            )

    own_amp = pltpu.make_async_copy(amp, both.at[core], amp_sem.at[0])
    own_amp.start()
    own_piece = pltpu.make_async_copy(
        panel.at[:, pl.ds(pl.multiple_of(r * strip, strip), strip), :], piece_in.at[r], amp_sem.at[1]
    )
    own_piece.start()

    barrier = pltpu.get_barrier_semaphore()

    def greet(d, carry):
        pl.semaphore_signal(barrier, 1, device_id=(lax.rem(r + d, rows_of), c), device_id_type=MESH)
        return carry

    lax.fori_loop(1, rows_of, greet, 0)
    for step in (1, -1, 2, -2):
        pl.semaphore_signal(barrier, 1, device_id=(r, at_chip(step)), device_id_type=MESH)
    partner = chip * 2 + 1 - core
    pl.semaphore_signal(barrier, 1, device_id=(r, partner), device_id_type=MESH)
    pl.semaphore_wait(barrier, rows_of - 1 + 5)

    def piece_copies(d):
        peer = lax.rem(r + d, rows_of)
        return (
            pltpu.make_async_remote_copy(
                src_ref=panel.at[:, pl.ds(pl.multiple_of(peer * strip, strip), strip), :],
                dst_ref=piece_in.at[r],
                send_sem=a2a_send.at[0, d],
                recv_sem=a2a_recv.at[0, d],
                device_id=(peer, c),
                device_id_type=MESH,
            ),
            pltpu.make_async_remote_copy(
                src_ref=meta,
                dst_ref=meta_in.at[r],
                send_sem=a2a_send.at[1, d],
                recv_sem=a2a_recv.at[1, d],
                device_id=(peer, c),
                device_id_type=MESH,
            ),
        )

    def send_pieces(d, carry):
        for copy in piece_copies(d):
            copy.start()
        return carry

    lax.fori_loop(1, rows_of, send_pieces, 0)

    swaps = (
        pltpu.make_async_remote_copy(
            src_ref=maskv.at[core], dst_ref=maskv.at[core], send_sem=amp_send.at[0], recv_sem=amp_recv.at[0],
            device_id=(r, partner), device_id_type=MESH,
        ),
        pltpu.make_async_remote_copy(
            src_ref=amp, dst_ref=both.at[core], send_sem=amp_send.at[1], recv_sem=amp_recv.at[1],
            device_id=(r, partner), device_id_type=MESH,
        ),
    )
    for copy in swaps:
        copy.start()

    def wait_pieces(d, carry):
        for copy in piece_copies(d):
            copy.wait_recv()
        return carry

    own_piece.wait()
    lax.fori_loop(1, rows_of, wait_pieces, 0)

    chosen = []
    for even_step, odd_step in ((2, 3), (1, 2), (0, 1), (3, 0)):
        chosen.append(owner_ref[even_step * (1 - core) + odd_step * core, 0])
    for slot in (0, 1):
        q_out[slot] = piece_in[chosen[slot]]
        fac_out[slot] = meta_in[chosen[slot]]
    p_b[r, 0] = piece_in[chosen[2]]
    fac_b[0] = meta_in[chosen[2]]

    @pl.when(core == 0)
    def _():
        q_out[2] = piece_in[chosen[3]]
        fac_out[2] = meta_in[chosen[3]]

    @pl.when(core == 1)
    def _():
        p_b[r, 1] = piece_in[chosen[3]]
        fac_b[1] = meta_in[chosen[3]]

    shift_one = (
        pltpu.make_async_remote_copy(
            src_ref=q_out.at[pl.ds(0, 2)], dst_ref=p_a.at[r], send_sem=shift_send.at[0], recv_sem=shift_recv.at[0],
            device_id=(r, at_chip(-1)), device_id_type=MESH,
        ),
        pltpu.make_async_remote_copy(
            src_ref=fac_out.at[pl.ds(0, 2)], dst_ref=fac_a, send_sem=shift_send.at[1], recv_sem=shift_recv.at[1],
            device_id=(r, at_chip(-1)), device_id_type=MESH,
        ),
    )
    shift_two = (
        pltpu.make_async_remote_copy(
            src_ref=q_out.at[2], dst_ref=p_b.at[r, 1], send_sem=shift_send.at[2], recv_sem=shift_recv.at[2],
            device_id=(r, at_chip(-2)), device_id_type=MESH,
        ),
        pltpu.make_async_remote_copy(
            src_ref=fac_out.at[2], dst_ref=fac_b.at[1], send_sem=shift_send.at[3], recv_sem=shift_recv.at[3],
            device_id=(r, at_chip(-2)), device_id_type=MESH,
        ),
    )
    for copy in shift_one:
        copy.start()

    @pl.when(core == 0)
    def _():
        for copy in shift_two:
            copy.start()

    def ring_copy(buf, send, recv, chain, way, step):
        half = lax.rem(y + chain, 2)
        if way == 0:
            block_z, to_z = lax.rem(z - (step - 1) + depth_z, depth_z), lax.rem(z + 1, depth_z)
        else:
            block_z, to_z = lax.rem(z + (step - 1), depth_z), lax.rem(z - 1 + depth_z, depth_z)
        held = buf.at[half * depth_z + block_z]
        return pltpu.make_async_remote_copy(
            src_ref=held, dst_ref=held, send_sem=send.at[chain, way, step], recv_sem=recv.at[chain, way, step],
            device_id=(y * depth_z + to_z, c), device_id_type=MESH,
        )

    def cross_copy(buf, send, recv):
        return pltpu.make_async_remote_copy(
            src_ref=buf.at[r], dst_ref=buf.at[r], send_sem=send.at[0, 0, 0], recv_sem=recv.at[0, 0, 0],
            device_id=(lax.rem(r + depth_z, rows_of), c), device_id_type=MESH,
        )

    reach = (depth_z // 2, (depth_z - 1) // 2)

    def ring_received(buf, send, recv, chain, way, step):
        half = lax.rem(y + chain, 2)
        block_z = lax.rem(z - step + depth_z, depth_z) if way == 0 else lax.rem(z + step, depth_z)
        held = buf.at[half * depth_z + block_z]
        return pltpu.make_async_remote_copy(
            src_ref=held, dst_ref=held, send_sem=send.at[chain, way, step], recv_sem=recv.at[chain, way, step],
            device_id=(r, partner), device_id_type=MESH,
        )

    def ring_step(buf, send, recv, step):
        for chain in (0, 1):
            if step == 1 and chain == 1:
                cross_copy(buf, send, recv).wait_recv()
            for way in (0, 1):
                if 1 < step <= reach[way] + 1:
                    ring_received(buf, send, recv, chain, way, step - 1).wait_recv()
                if step <= reach[way]:
                    ring_copy(buf, send, recv, chain, way, step).start()

    def ring_drain(buf, send, recv):
        cross_copy(buf, send, recv).wait_send()
        for chain in (0, 1):
            for way in (0, 1):
                for step in range(1, reach[way] + 1):
                    ring_copy(buf, send, recv, chain, way, step).wait_send()

    def assemble(fac, strips, weights):
        for slot in (0, 1):
            factors = []
            for k in range(2):
                for t in range(tiles):
                    f = jnp.broadcast_to(fac[slot, k * tiles + t : k * tiles + t + 1, :], (strip, 128))
                    factors.append(jnp.concatenate([f] * (tile // 128), axis=1).astype(BF16))

            def put(i, carry):
                first, second = strips[i, slot, 0], strips[i, slot, 1]
                for t in range(tiles):
                    weights[slot, pl.ds(pl.multiple_of(t * tile + i * strip, strip), strip), :] = (
                        first * factors[t] + second * factors[tiles + t]
                    )
                return carry

            lax.fori_loop(0, rows_of, put, 0)

    def masked(group, i):
        m = jnp.broadcast_to(maskv[group, pl.ds(i, 1), :], (16, width)).astype(BF16)
        a = both[group, pl.ds(pl.multiple_of(i * block, block), block), :]
        return (a.reshape(block // 16, 16, width) * m[None]).reshape(block, width)

    def coded(x):
        peak = jnp.maximum(jnp.max(jnp.abs(x), axis=0, keepdims=True), TINY)
        return jnp.round(x * (TOP / peak)).astype(jnp.int32).astype(LINK), peak * (1.0 / TOP)

    def rows(i):
        return pl.ds(pl.multiple_of(i * block, block), block)

    one_chip = 1 - 2 * y_lo * (1 - core)

    def flow_one(i):
        where = (r, at_chip(one_chip))
        return (
            pltpu.make_async_remote_copy(
                src_ref=s_out.at[rows(i)], dst_ref=r_one.at[rows(i)], send_sem=one_send.at[0, i],
                recv_sem=one_recv.at[0, i], device_id=where, device_id_type=MESH,
            ),
            pltpu.make_async_remote_copy(
                src_ref=s_scale.at[i], dst_ref=r_one_scale.at[i], send_sem=one_send.at[1, i],
                recv_sem=one_recv.at[1, i], device_id=where, device_id_type=MESH,
            ),
        )

    def flow_two(i):
        where = (r, at_chip(2))
        return (
            pltpu.make_async_remote_copy(
                src_ref=t_out.at[rows(i)], dst_ref=r_two.at[rows(i)], send_sem=two_send.at[0, i],
                recv_sem=two_recv.at[0, i], device_id=where, device_id_type=MESH,
            ),
            pltpu.make_async_remote_copy(
                src_ref=t_scale.at[i], dst_ref=r_two_scale.at[i], send_sem=two_send.at[1, i],
                recv_sem=two_recv.at[1, i], device_id=where, device_id_type=MESH,
            ),
        )

    ring_a = (p_a, ring_send_a, ring_recv_a)
    ring_b = (p_b, ring_send_b, ring_recv_b)
    for copy in shift_one:
        copy.wait_recv()
    cross_copy(*ring_a).start()
    for step in range(1, reach[0] + 2):
        ring_step(*ring_a, step)

    @pl.when(core == 0)
    def _():
        for copy in shift_two:
            copy.wait_recv()

    cross_copy(*ring_b).start()
    assemble(fac_a, p_a, w_a)
    own_amp.wait()
    for copy in swaps:
        copy.wait_recv()

    def outward(i, carry):
        x = jnp.dot(masked(0, i), w_a[0], preferred_element_type=F32)
        x = x + jnp.dot(masked(1, i), w_a[1], preferred_element_type=F32)
        code, scale = coded(x)
        s_out[rows(i)] = code
        s_scale[i] = jnp.broadcast_to(scale, (8, tile))
        for copy in flow_one(i):
            copy.start()
        return carry

    stages = reach[0] + 1
    done = 0
    for step in range(1, stages + 1):
        ring_step(*ring_b, step)
        upto = blocks * step // stages
        lax.fori_loop(done, upto, outward, 0)
        done = upto
    assemble(fac_b, p_b, w_b)

    def received(buf, scale, i):
        return buf[rows(i)].astype(jnp.int32).astype(F32) * scale[i][0:1]

    def inward(i, carry):
        m_even = jnp.dot(masked(0, i), w_b[0], preferred_element_type=F32)
        m_odd = jnp.dot(masked(1, i), w_b[1], preferred_element_type=F32)

        @pl.when(core == 1)
        def _():
            local[rows(i)] = m_even + m_odd

        @pl.when(core == 0)
        def _():
            local[rows(i)] = m_even
            t_own[...] = m_odd

            @pl.when(y_lo == 0)
            def _():
                for copy in flow_one(i):
                    copy.wait_recv()
                t_own[...] = t_own[...] + received(r_one, r_one_scale, i)

            code, scale = coded(t_own[...])
            t_out[rows(i)] = code
            t_scale[i] = jnp.broadcast_to(scale, (8, tile))
            for copy in flow_two(i):
                copy.start()

        return carry

    lax.fori_loop(0, blocks, inward, 0)

    def result_copy(i):
        return pltpu.make_async_copy(result.at[rows(i)], out.at[rows(i)], out_sem.at[i])

    def finish(i, carry):
        @pl.when(y_lo + core > 0)
        def _():
            for copy in flow_one(i):
                copy.wait_recv()
            local[rows(i)] = local[rows(i)] + received(r_one, r_one_scale, i)

        @pl.when(core == 0)
        def _():
            for copy in flow_two(i):
                copy.wait_recv()
            local[rows(i)] = local[rows(i)] + received(r_two, r_two_scale, i)

        result[rows(i)] = local[rows(i)].astype(BF16)
        result_copy(i).start()
        return carry

    lax.fori_loop(0, blocks, finish, 0)

    def drain_pieces(d, carry):
        for copy in piece_copies(d):
            copy.wait_send()
        return carry

    lax.fori_loop(1, rows_of, drain_pieces, 0)
    for copy in swaps + shift_one:
        copy.wait_send()

    @pl.when(core == 0)
    def _():
        for copy in shift_two:
            copy.wait_send()

    ring_drain(*ring_a)
    ring_drain(*ring_b)

    def drain_flows(i, carry):
        for copy in flow_one(i):
            copy.wait_send()

        @pl.when(core == 0)
        def _():
            for copy in flow_two(i):
                copy.wait_send()

        result_copy(i).wait()
        return carry

    lax.fori_loop(0, blocks, drain_flows, 0)


def shards(rows_of, cols_of, amplitudes, pair_mask, integrals, tile_list, tile_count, owner):
    count, width = amplitudes.shape
    tile = integrals.shape[-1]
    blocks, tiles = pair_mask.shape
    block = count // blocks
    strip = tile // rows_of
    reach = rows_of // 4
    dma = pltpu.SemaphoreType.DMA
    vmem = pltpu.VMEM
    smem = pl.BlockSpec(memory_space=pltpu.SMEM)
    away = pl.BlockSpec(memory_space=pl.ANY)
    code = vmem((count, tile), LINK)
    scale = vmem((blocks, 8, tile), F32)
    strips = vmem((rows_of, 2, 2, strip, tile), BF16)
    return pl.pallas_call(
        functools.partial(kernel, rows_of, cols_of),
        out_shape=jax.ShapeDtypeStruct((count, tile), BF16),
        in_specs=[smem, smem, smem, smem, away, away],
        out_specs=away,
        scratch_shapes=[
            vmem((2, count, width), BF16),
            vmem((2, blocks, width), F32),
            vmem((8, 128), F32),
            vmem((rows_of, 8, 128), F32),
            vmem((rows_of, 2, strip, tile), BF16),
            vmem((3, 8, 128), F32),
            vmem((2, 8, 128), F32),
            vmem((2, 8, 128), F32),
            vmem((3, 2, strip, tile), BF16),
            strips,
            strips,
            vmem((2, width, tile), BF16),
            vmem((2, width, tile), BF16),
            vmem((count, tile), F32),
            vmem((block, tile), F32),
            code, scale, code, scale, code, scale, code, scale,
            vmem((count, tile), BF16),
            dma((2,)), dma((2,)), dma((2,)),
            dma((2, rows_of)), dma((2, rows_of)),
            dma((4,)), dma((4,)),
            dma((2, 2, reach + 1)), dma((2, 2, reach + 1)),
            dma((2, 2, reach + 1)), dma((2, 2, reach + 1)),
            dma((2, blocks)), dma((2, blocks)),
            dma((2, blocks)), dma((2, blocks)),
            dma((blocks,)),
        ],
        compiler_params=pltpu.CompilerParams(
            collective_id=0, has_side_effects=True, vmem_limit_bytes=56 * 1024 * 1024
        ),
    )(owner, tile_list, tile_count, pair_mask, amplitudes, integrals.reshape(integrals.shape[2:]))


def solution(mesh):
    return jax.shard_map(
        functools.partial(shards, mesh.shape["row"], mesh.shape["col"]),
        mesh=mesh,
        in_specs=(
            P("row", "col"),
            P("row", "col"),
            P("row", "col", None, None, None),
            P("row", "col", None),
            P("row", "col"),
            P(None, "col"),
        ),
        out_specs=P("row", "col"),
        check_vma=False,
    )
```

time: 334 us -> 104 us (0.31)
  the two profiles are of different devices: /device:TPU:2 before, /device:TPU:8 now
where the time goes in v1:
time: 104 us
  Pallas kernels  97.7 us (94%)
  local copies, waits for them, and re-layouts  5.32 us (5%)
    pallas_call x1, Pallas kernels, shards(): pl.pallas_call(functools.partial(kernel, rows_of, cols_of), out_shape=jax...  97.7 us
    unnamed x3, local copies, waits for them, and re-layouts  5.32 us

profile of v1, /device:TPU:8, one launch (start us, length us, event | category | flops | bytes accessed | tf_op | source)
XLA Modules:
  0.0 103.7 jit_solution(2519686527298100741)
XLA Ops:
  0.7 1.3 %copy.7.owner_ref = s32[4,1]{1,0:T(4,128)} copy(s32[4,1]{0,1:T(1,128)} %param.11) | data formatting | bytes 32 | tf_op args[5]
  2.0 1.4 %copy.8.mask_ref = s32[12,3]{1,0:T(8,128)} copy(s32[12,3]{0,1:T(4,128)} %param.7) | data formatting | bytes 288 | tf_op args[1]
  3.3 97.7 %shard_map.64 = bf16[3072,256]{1,0:T(8,128)(2,1)} custom-call(s32[4,1]{1,0:T(4,128)} %copy.7.owner_ref, s32[1,1,2]{2,1,0:T(1,128)} %list_ref.1, s32[1,1]{1,0:T(1,128)S(6)} %copy.10.count_ref, s32[12,3]{1,0:T(8,128)} %copy.8.mask_ref, bf16[3072,768]{1,0:T(8,128)(2,1)} %amp.1, bf16[2,256,256]{2,1,0:T(8,128)(2,1)} %bitcast.1), custom_call_target="tpu_custom_call" | custom-call | tf_op jit(solution)/shard_map/pallas_call | solution.py:411
  101.0 2.7 %copy.11 = bf16[3072,256]{1,0:T(8,128)(2,1)} copy(bf16[3072,256]{1,0:T(8,128)(2,1)} %shard_map.64) | data formatting | bytes 3145728

commit v2 on v1

v2 whole, which is shorter than its diff:
```python
import functools

import jax
import jax.numpy as jnp
from jax import lax
from jax.experimental import pallas as pl
from jax.experimental.pallas import tpu as pltpu
from jax.sharding import PartitionSpec as P

MESH = pl.DeviceIdType.MESH
F32 = jnp.float32
BF16 = jnp.bfloat16
LINK = jnp.int16
TOP = 32767.0
TINY = 1e-33
AHEAD = 2
LAG = 4


def kernel(
    rows_of, cols_of, owner_ref, list_ref, count_ref, mask_ref, amp, panel, out,
    both, maskv, ahead, mask_ahead, meta, meta_in, piece_in, half_s, half_f, got_s, got_f, fac_a, fac_t, fac_l, fac_c,
    p_a, p_t, p_l, p_c, w_a, w_t, w_l, w_c, local, t_own, s_out, s_scale, r_one, r_one_scale, t_out, t_scale, r_two, r_two_scale, result,
    amp_sem, amp_send, amp_recv, ahead_send, ahead_recv, pass_send, pass_recv,
    a2a_send, a2a_recv, shift_send, shift_recv, ring_send, ring_recv, one_send, one_recv, two_send, two_recv, out_sem,
):
    r, c = lax.axis_index("row"), lax.axis_index("col")
    depth_z = rows_of // 2
    chips = cols_of // 2
    y, z = r // depth_z, r % depth_z
    chip, core = c // 2, c % 2
    y_lo = chip % 2
    tile = panel.shape[-1]
    strip = tile // depth_z
    blocks, tiles = mask_ref.shape
    block = amp.shape[0] // blocks
    width = amp.shape[1]

    def at_chip(step, same_core=True):
        return lax.rem(chip + step + chips, chips) * 2 + core

    row_id = lax.broadcasted_iota(jnp.int32, (8, 128), 0)
    flags = jnp.zeros((8, 128), F32)
    for k in range(2):
        live = jnp.where(k < count_ref[0, 0], k * tiles + list_ref[0, 0, k], -1)
        flags = flags + jnp.where(row_id == live, 1.0, 0.0)
    meta[...] = flags
    meta_in[z] = flags
    for t in range(tiles):
        maskv[core, :, t * tile : (t + 1) * tile] = jnp.broadcast_to(
            mask_ref[:, t : t + 1].astype(F32), (blocks, tile)
        )

    own_amp = pltpu.make_async_copy(amp, both.at[core], amp_sem.at[0])
    own_amp.start()
    own_piece = pltpu.make_async_copy(
        panel.at[:, pl.ds(pl.multiple_of(z * strip, strip), strip), :], piece_in.at[z], amp_sem.at[1]
    )
    own_piece.start()

    barrier = pltpu.get_barrier_semaphore()

    across = lax.rem(r + depth_z, rows_of)

    def z_peer(d):
        return lax.rem(z + d, depth_z)

    def greet(d, carry):
        pl.semaphore_signal(barrier, 1, device_id=(y * depth_z + z_peer(d), c), device_id_type=MESH)
        return carry

    lax.fori_loop(1, depth_z, greet, 0)
    for step in (1, -1, 2, -2):
        for row in (r, across):
            pl.semaphore_signal(barrier, 1, device_id=(row, at_chip(step)), device_id_type=MESH)
    partner = chip * 2 + 1 - core
    pl.semaphore_signal(barrier, 1, device_id=(across, c), device_id_type=MESH)
    pl.semaphore_signal(barrier, 1, device_id=(r, partner), device_id_type=MESH)
    pl.semaphore_wait(barrier, depth_z - 1 + 10)

    def piece_copies(d):
        peer = z_peer(d)
        return (
            pltpu.make_async_remote_copy(
                src_ref=panel.at[:, pl.ds(pl.multiple_of(peer * strip, strip), strip), :],
                dst_ref=piece_in.at[z],
                send_sem=a2a_send.at[0, d],
                recv_sem=a2a_recv.at[0, d],
                device_id=(y * depth_z + peer, c),
                device_id_type=MESH,
            ),
            pltpu.make_async_remote_copy(
                src_ref=meta,
                dst_ref=meta_in.at[z],
                send_sem=a2a_send.at[1, d],
                recv_sem=a2a_recv.at[1, d],
                device_id=(y * depth_z + peer, c),
                device_id_type=MESH,
            ),
        )

    def send_pieces(d, carry):
        for copy in piece_copies(d):
            copy.start()
        return carry

    lax.fori_loop(1, depth_z, send_pieces, 0)

    swaps = (
        pltpu.make_async_remote_copy(
            src_ref=maskv.at[core], dst_ref=maskv.at[core], send_sem=amp_send.at[0], recv_sem=amp_recv.at[0],
            device_id=(r, partner), device_id_type=MESH,
        ),
        pltpu.make_async_remote_copy(
            src_ref=amp, dst_ref=both.at[core], send_sem=amp_send.at[1], recv_sem=amp_recv.at[1],
            device_id=(r, partner), device_id_type=MESH,
        ),
    )
    for copy in swaps:
        copy.start()

    def rows(i):
        return pl.ds(pl.multiple_of(i * block, block), block)

    def ahead_copy(i):
        return pltpu.make_async_remote_copy(
            src_ref=amp.at[rows(i)], dst_ref=ahead.at[core, rows(i)], send_sem=ahead_send.at[i], recv_sem=ahead_recv.at[i],
            device_id=(r, at_chip(1)), device_id_type=MESH,
        )

    def pass_copy(i):
        return pltpu.make_async_remote_copy(
            src_ref=ahead.at[core, rows(i)], dst_ref=ahead.at[core, rows(i)], send_sem=pass_send.at[i],
            recv_sem=pass_recv.at[i], device_id=(r, partner), device_id_type=MESH,
        )

    mask_copy = pltpu.make_async_remote_copy(
        src_ref=maskv.at[core], dst_ref=mask_ahead.at[core], send_sem=ahead_send.at[AHEAD], recv_sem=ahead_recv.at[AHEAD],
        device_id=(r, at_chip(1)), device_id_type=MESH,
    )
    mask_pass = pltpu.make_async_remote_copy(
        src_ref=mask_ahead.at[core], dst_ref=mask_ahead.at[core], send_sem=pass_send.at[AHEAD],
        recv_sem=pass_recv.at[AHEAD], device_id=(r, partner), device_id_type=MESH,
    )
    mask_copy.start()
    ahead_copy(0).start()

    def wait_pieces(d, carry):
        for copy in piece_copies(d):
            copy.wait_recv()
        return carry

    own_piece.wait()
    lax.fori_loop(1, depth_z, wait_pieces, 0)

    def chosen(even_step, odd_step):
        holder = owner_ref[pl.ds(even_step * (1 - core) + odd_step * core, 1), :] - y * depth_z
        wide = jnp.broadcast_to(holder, (strip, tile))
        small = jnp.broadcast_to(holder, (8, 128))
        first, second, factors = jnp.zeros((strip, tile), BF16), jnp.zeros((strip, tile), BF16), jnp.zeros((8, 128), F32)
        for j in range(depth_z):
            named = jnp.where(wide == j, 1.0, 0.0).astype(BF16)
            first = first + named * piece_in[j, 0]
            second = second + named * piece_in[j, 1]
            factors = factors + jnp.where(small == j, meta_in[j], 0.0)
        return first, second, factors

    for slot, steps in enumerate(((2, 3), (1, 2), (0, 1), (3, 0))):
        half_s[slot, 0], half_s[slot, 1], half_f[slot] = chosen(*steps)

    def halves(first, count, landing, step, n):
        out = []
        for m, row in enumerate((r, across)):
            for k, (src, dst) in enumerate(((half_s, got_s), (half_f, got_f))):
                out.append(
                    pltpu.make_async_remote_copy(
                        src_ref=src.at[pl.ds(first, count)], dst_ref=dst.at[m, pl.ds(landing, count)],
                        send_sem=shift_send.at[n, m, k], recv_sem=shift_recv.at[n, m, k],
                        device_id=(row, at_chip(step)), device_id_type=MESH,
                    )
                )
        return out

    back_one = halves(0, 2, 0, -1, 0)
    stay = halves(0, 3, 2, 0, 1)[2:]
    stay_odd = halves(3, 1, 5, 0, 2)[2:]
    back_two = halves(3, 1, 5, -2, 2)
    for copy in back_one:
        copy.start()

    @pl.when(core == 0)
    def _():
        for copy in back_two:
            copy.start()

    for copy in stay:
        copy.start()

    @pl.when(core == 1)
    def _():
        for copy in stay_odd:
            copy.start()

    turn = 1 - 2 * core
    hops = [(0, 1), (0, -1)]
    if depth_z > 4:
        hops += [(0, 2), (0, -2), (2, 1), (-2, -1), (2 * turn, 2 * turn)]
    else:
        hops += [(0, 2 * turn)]
    direct = 4 if depth_z > 4 else 3

    def strips_of(which, back):
        return (p_a, p_t, p_l, p_c)[which].at[lax.rem(z - back + depth_z, depth_z)]

    def hop_copy(which, n):
        behind, on = hops[n]
        held = strips_of(which, behind)
        return pltpu.make_async_remote_copy(
            src_ref=held, dst_ref=held, send_sem=ring_send.at[which, n], recv_sem=ring_recv.at[which, n],
            device_id=(y * depth_z + lax.rem(z + on + depth_z, depth_z), c), device_id_type=MESH,
        )

    def hop_received(which, n):
        behind, on = hops[n]
        held = strips_of(which, behind + on)
        pltpu.make_async_remote_copy(
            src_ref=held, dst_ref=held, send_sem=ring_send.at[which, n], recv_sem=ring_recv.at[which, n],
            device_id=(r, partner), device_id_type=MESH,
        ).wait_recv()

    def ring_first(which):
        for n in range(direct):
            hop_copy(which, n).start()

    def ring_second(which):
        if direct < len(hops):
            hop_received(which, 2)
            hop_received(which, 3)
        for n in range(direct, len(hops)):
            hop_copy(which, n).start()

    def ring_rest(which):
        for n in range(len(hops)):
            if direct == len(hops) or n not in (2, 3):
                hop_received(which, n)

    def ring_drain(which):
        for n in range(len(hops)):
            hop_copy(which, n).wait_send()

    def assemble(fac, strips, weights):
        for slot in range(weights.shape[0]):
            factors = []
            for k in range(2):
                for t in range(tiles):
                    f = jnp.broadcast_to(fac[slot, k * tiles + t : k * tiles + t + 1, :], (strip, 128))
                    factors.append(jnp.concatenate([f] * (tile // 128), axis=1).astype(BF16))

            def put(i, carry):
                first, second = strips[i, slot, 0], strips[i, slot, 1]
                for t in range(tiles):
                    weights[slot, pl.ds(pl.multiple_of(t * tile + i * strip, strip), strip), :] = (
                        first * factors[t] + second * factors[tiles + t]
                    )
                return carry

            lax.fori_loop(0, depth_z, put, 0)

    def masked(group, i, mask=maskv, held=both):
        m = jnp.broadcast_to(mask[group, pl.ds(i, 1), :], (16, width)).astype(BF16)
        a = held[group, rows(i), :]
        return (a.reshape(block // 16, 16, width) * m[None]).reshape(block, width)

    def coded(x):
        peak = jnp.maximum(jnp.max(jnp.abs(x), axis=0, keepdims=True), TINY)
        return jnp.round(x * (TOP / peak)).astype(jnp.int32).astype(LINK), peak * (1.0 / TOP)

    one_chip = 1 - 2 * y_lo * (1 - core)

    def flow_one(i):
        where = (r, at_chip(one_chip))
        return (
            pltpu.make_async_remote_copy(
                src_ref=s_out.at[rows(i)], dst_ref=r_one.at[rows(i)], send_sem=one_send.at[0, i],
                recv_sem=one_recv.at[0, i], device_id=where, device_id_type=MESH,
            ),
            pltpu.make_async_remote_copy(
                src_ref=s_scale.at[i], dst_ref=r_one_scale.at[i], send_sem=one_send.at[1, i],
                recv_sem=one_recv.at[1, i], device_id=where, device_id_type=MESH,
            ),
        )

    def flow_two(i):
        where = (r, at_chip(2))
        return (
            pltpu.make_async_remote_copy(
                src_ref=t_out.at[rows(i)], dst_ref=r_two.at[rows(i)], send_sem=two_send.at[0, i],
                recv_sem=two_recv.at[0, i], device_id=where, device_id_type=MESH,
            ),
            pltpu.make_async_remote_copy(
                src_ref=t_scale.at[i], dst_ref=r_two_scale.at[i], send_sem=two_send.at[1, i],
                recv_sem=two_recv.at[1, i], device_id=where, device_id_type=MESH,
            ),
        )

    for copy in back_one:
        copy.wait_recv()
    for slot in (0, 1):
        p_a[z, slot] = got_s[0, slot] + got_s[1, slot]
        fac_a[slot] = got_f[0, slot] + got_f[1, slot]
    ring_first(0)

    @pl.when(core == 0)
    def _():
        for copy in back_two:
            copy.wait_recv()
        p_t[z, 0] = got_s[0, 5] + got_s[1, 5]
        fac_t[0] = got_f[0, 5] + got_f[1, 5]

    @pl.when(core == 1)
    def _():
        for copy in stay_odd:
            copy.wait_recv()
        p_t[z, 0] = half_s[3] + got_s[1, 5]
        fac_t[0] = half_f[3] + got_f[1, 5]

    for copy in stay:
        copy.wait_recv()
    for i in range(1, AHEAD):
        ahead_copy(i).start()
    p_l[z, 0] = half_s[2] + got_s[1, 4]
    fac_l[0] = half_f[2] + got_f[1, 4]
    for slot in (0, 1):
        p_c[z, slot] = half_s[slot] + got_s[1, 2 + slot]
        fac_c[slot] = half_f[slot] + got_f[1, 2 + slot]
    ring_second(0)
    ring_first(1)
    ring_rest(0)
    assemble(fac_a, p_a, w_a)
    own_amp.wait()
    for copy in swaps:
        copy.wait_recv()

    def outward(i):
        x = jnp.dot(masked(0, i), w_a[0], preferred_element_type=F32)
        x = x + jnp.dot(masked(1, i), w_a[1], preferred_element_type=F32)
        code, scale = coded(x)
        s_out[rows(i)] = code
        s_scale[i] = jnp.broadcast_to(scale, (8, tile))
        for copy in flow_one(i):
            copy.start()

    def received(buf, scale, i):
        return buf[rows(i)].astype(jnp.int32).astype(F32) * scale[i][0:1]

    def send_two(i, x):
        code, scale = coded(x)
        t_out[rows(i)] = code
        t_scale[i] = jnp.broadcast_to(scale, (8, tile))
        for copy in flow_two(i):
            copy.start()

    def odd_term(i, direct):
        x = jnp.dot(masked(1, i), w_t[0], preferred_element_type=F32)
        t_own[rows(i)] = x

        @pl.when((core == 0) if direct else ((core == 0) & (y_lo == 1)))
        def _():
            send_two(i, x)

    def relay(i):
        @pl.when((core == 0) & (y_lo == 0))
        def _():
            for copy in flow_one(i):
                copy.wait_recv()
            send_two(i, t_own[rows(i)] + received(r_one, r_one_scale, i))

    def result_copy(i):
        return pltpu.make_async_copy(result.at[rows(i)], out.at[rows(i)], out_sem.at[i])

    def here(i):
        x = jnp.dot(masked(0, i), w_l[0], preferred_element_type=F32)

        @pl.when(core == 1)
        def _():
            local[rows(i)] = x + t_own[rows(i)]

        @pl.when(core == 0)
        def _():
            local[rows(i)] = x

    def finish(i, early):
        if not early:

            @pl.when(y_lo + core > 0)
            def _():
                for copy in flow_one(i):
                    copy.wait_recv()
                local[rows(i)] = local[rows(i)] + received(r_one, r_one_scale, i)

        @pl.when(core == 0)
        def _():
            for copy in flow_two(i):
                copy.wait_recv()
            local[rows(i)] = local[rows(i)] + received(r_two, r_two_scale, i)

        result[rows(i)] = local[rows(i)].astype(BF16)
        result_copy(i).start()

    def each(first, last, *calls):
        def body(i, carry):
            for call in calls:
                call(i)
            return carry

        lax.fori_loop(first, last, body, 0)

    late = blocks - AHEAD
    cuts = [AHEAD + late * k // 4 for k in range(5)]
    each(cuts[0], cuts[1], outward)
    ring_second(1)
    for which in (2, 3):
        ring_first(which)
    each(cuts[1], cuts[2], outward)
    ring_rest(1)
    assemble(fac_t, p_t, w_t)
    each(0, AHEAD, lambda i: odd_term(i, True))
    each(cuts[0], cuts[1], lambda i: odd_term(i, False))
    each(cuts[2], cuts[3], outward)
    for which in (2, 3):
        ring_second(which)
    each(cuts[1], cuts[2], lambda i: odd_term(i, False))
    each(cuts[3], cuts[4], outward)
    mask_copy.wait_recv()
    mask_pass.start()
    for i in range(AHEAD):
        ahead_copy(i).wait_recv()
        pass_copy(i).start()
    each(cuts[2], cuts[4], lambda i: odd_term(i, False))
    each(cuts[0], cuts[1], relay)
    ring_rest(2)
    assemble(fac_l, p_l, w_l)
    each(0, blocks, here)
    each(cuts[1], cuts[2], relay)
    ring_rest(3)
    assemble(fac_c, p_c, w_c)
    mask_pass.wait_recv()

    def from_ahead(i):
        pass_copy(i).wait_recv()
        local[rows(i)] = (
            local[rows(i)]
            + jnp.dot(masked(0, i, mask_ahead, ahead), w_c[0], preferred_element_type=F32)
            + jnp.dot(masked(1, i, mask_ahead, ahead), w_c[1], preferred_element_type=F32)
        )
        finish(i, True)

    each(0, AHEAD, from_ahead)
    ready = cuts[2] - LAG
    assert ready >= AHEAD
    each(AHEAD, ready, lambda i: finish(i, False))
    each(cuts[2], blocks, relay, lambda i: finish(i - LAG, False))
    each(blocks - LAG, blocks, lambda i: finish(i, False))

    def drain_pieces(d, carry):
        for copy in piece_copies(d):
            copy.wait_send()
        return carry

    lax.fori_loop(1, depth_z, drain_pieces, 0)
    for copy in list(swaps) + back_one + stay:
        copy.wait_send()

    @pl.when(core == 0)
    def _():
        for copy in back_two:
            copy.wait_send()

    @pl.when(core == 1)
    def _():
        for copy in stay_odd:
            copy.wait_send()

    for which in (0, 1, 2, 3):
        ring_drain(which)
    for copy in (mask_copy, mask_pass):
        copy.wait_send()
    for i in range(AHEAD):
        ahead_copy(i).wait_send()
        pass_copy(i).wait_send()

    def drain_one(i, carry):
        for copy in flow_one(i):
            copy.wait_send()
        return carry

    lax.fori_loop(AHEAD, blocks, drain_one, 0)

    def drain_two(i, carry):
        @pl.when(core == 0)
        def _():
            for copy in flow_two(i):
                copy.wait_send()

        result_copy(i).wait()
        return carry

    lax.fori_loop(0, blocks, drain_two, 0)


def shards(rows_of, cols_of, amplitudes, pair_mask, integrals, tile_list, tile_count, owner):
    count, width = amplitudes.shape
    tile = integrals.shape[-1]
    blocks, tiles = pair_mask.shape
    block = count // blocks
    depth_z = rows_of // 2
    strip = tile // depth_z
    hops = 7 if depth_z > 4 else 3
    dma = pltpu.SemaphoreType.DMA
    vmem = pltpu.VMEM
    near = pl.BlockSpec(memory_space=pltpu.VMEM)
    smem = pl.BlockSpec(memory_space=pltpu.SMEM)
    away = pl.BlockSpec(memory_space=pl.ANY)
    code = vmem((count, tile), LINK)
    scale = vmem((blocks, 8, tile), F32)

    def strips(slots):
        return vmem((depth_z, slots, 2, strip, tile), BF16)

    return pl.pallas_call(
        functools.partial(kernel, rows_of, cols_of),
        out_shape=jax.ShapeDtypeStruct((count, tile), BF16),
        in_specs=[near, smem, smem, near, away, away],
        out_specs=away,
        scratch_shapes=[
            vmem((2, count, width), BF16),
            vmem((2, blocks, width), F32),
            vmem((2, AHEAD * block, width), BF16),
            vmem((2, blocks, width), F32),
            vmem((8, 128), F32),
            vmem((depth_z, 8, 128), F32),
            vmem((depth_z, 2, strip, tile), BF16),
            vmem((4, 2, strip, tile), BF16),
            vmem((4, 8, 128), F32),
            vmem((2, 6, 2, strip, tile), BF16),
            vmem((2, 6, 8, 128), F32),
            vmem((2, 8, 128), F32),
            vmem((1, 8, 128), F32),
            vmem((1, 8, 128), F32),
            vmem((2, 8, 128), F32),
            strips(2), strips(1), strips(1), strips(2),
            vmem((2, width, tile), BF16),
            vmem((1, width, tile), BF16),
            vmem((1, width, tile), BF16),
            vmem((2, width, tile), BF16),
            vmem((count, tile), F32),
            vmem((count, tile), F32),
            code, scale, code, scale, code, scale, code, scale,
            vmem((count, tile), BF16),
            dma((2,)), dma((2,)), dma((2,)),
            dma((AHEAD + 1,)), dma((AHEAD + 1,)), dma((AHEAD + 1,)), dma((AHEAD + 1,)),
            dma((2, depth_z)), dma((2, depth_z)),
            dma((3, 2, 2)), dma((3, 2, 2)),
            dma((4, hops)), dma((4, hops)),
            dma((2, blocks)), dma((2, blocks)),
            dma((2, blocks)), dma((2, blocks)),
            dma((blocks,)),
        ],
        compiler_params=pltpu.CompilerParams(
            collective_id=0, has_side_effects=True, vmem_limit_bytes=56 * 1024 * 1024
        ),
    )(owner, tile_list, tile_count, pair_mask, amplitudes, integrals.reshape(integrals.shape[2:]))


def solution(mesh):
    return jax.shard_map(
        functools.partial(shards, mesh.shape["row"], mesh.shape["col"]),
        mesh=mesh,
        in_specs=(
            P("row", "col"),
            P("row", "col"),
            P("row", "col", None, None, None),
            P("row", "col", None),
            P("row", "col"),
            P(None, "col"),
        ),
        out_specs=P("row", "col"),
        check_vma=False,
    )
```

time: 104 us -> 82.5 us (0.79)
  the two profiles are of different devices: /device:TPU:8 before, /device:TPU:2 now
where the time goes in v2:
time: 82.5 us; the launch traced here: 81.3 us
  Pallas kernels  75.3 us (91%)
  local copies, waits for them, and re-layouts  5.32 us (6%)
    pallas_call x1, Pallas kernels, shards(): pl.pallas_call(functools.partial(kernel, rows_of, cols_of), out_shape=jax...  75.3 us
    unnamed x3, local copies, waits for them, and re-layouts  5.32 us

profile of v2, /device:TPU:2, one launch (start us, length us, event | category | flops | bytes accessed | tf_op | source)
XLA Modules:
  0.0 81.3 jit_solution(4686763858609952268)
XLA Ops:
  0.7 1.3 %copy.7.owner_ref = s32[4,1]{1,0:T(4,128)} copy(s32[4,1]{0,1:T(1,128)} %param.11) | data formatting | bytes 32 | tf_op args[5]
  2.0 1.4 %copy.8.mask_ref = s32[12,3]{1,0:T(8,128)} copy(s32[12,3]{0,1:T(4,128)} %param.7) | data formatting | bytes 288 | tf_op args[1]
  3.3 75.3 %shard_map.64 = bf16[3072,256]{1,0:T(8,128)(2,1)} custom-call(s32[4,1]{1,0:T(4,128)} %copy.7.owner_ref, s32[1,1,2]{2,1,0:T(1,128)} %list_ref.1, s32[1,1]{1,0:T(1,128)S(6)} %copy.10.count_ref, s32[12,3]{1,0:T(8,128)} %copy.8.mask_ref, bf16[3072,768]{1,0:T(8,128)(2,1)} %amp.1, bf16[2,256,256]{2,1,0:T(8,128)(2,1)} %bitcast.1), custom_call_target="tpu_custom_call" | custom-call | tf_op jit(solution)/shard_map/pallas_call | solution.py:530
  78.6 2.7 %copy.11 = bf16[3072,256]{1,0:T(8,128)(2,1)} copy(bf16[3072,256]{1,0:T(8,128)(2,1)} %shard_map.64) | data formatting | bytes 3145728

commit v3 on v2

--- a/solution.py
+++ b/solution.py
@@ -14,6 +14,7 @@
 TOP = 32767.0
 TINY = 1e-33
 AHEAD = 2
+EARLY = 2
 LAG = 4
 
 
@@ -122,28 +123,32 @@
     def rows(i):
         return pl.ds(pl.multiple_of(i * block, block), block)
 
-    def ahead_copy(i):
+    def half_rows(n):
+        return pl.ds(pl.multiple_of(n * (block // 2), block // 2), block // 2)
+
+    def ahead_copy(n):
         return pltpu.make_async_remote_copy(
-            src_ref=amp.at[rows(i)], dst_ref=ahead.at[core, rows(i)], send_sem=ahead_send.at[i], recv_sem=ahead_recv.at[i],
-            device_id=(r, at_chip(1)), device_id_type=MESH,
-        )
-
-    def pass_copy(i):
+            src_ref=amp.at[half_rows(n)], dst_ref=ahead.at[core, half_rows(n)], send_sem=ahead_send.at[n],
+            recv_sem=ahead_recv.at[n], device_id=(r, at_chip(1)), device_id_type=MESH,
+        )
+
+    def pass_copy(n):
         return pltpu.make_async_remote_copy(
-            src_ref=ahead.at[core, rows(i)], dst_ref=ahead.at[core, rows(i)], send_sem=pass_send.at[i],
-            recv_sem=pass_recv.at[i], device_id=(r, partner), device_id_type=MESH,
+            src_ref=ahead.at[core, half_rows(n)], dst_ref=ahead.at[core, half_rows(n)], send_sem=pass_send.at[n],
+            recv_sem=pass_recv.at[n], device_id=(r, partner), device_id_type=MESH,
         )
 
     mask_copy = pltpu.make_async_remote_copy(
-        src_ref=maskv.at[core], dst_ref=mask_ahead.at[core], send_sem=ahead_send.at[AHEAD], recv_sem=ahead_recv.at[AHEAD],
+        src_ref=maskv.at[core], dst_ref=mask_ahead.at[core], send_sem=ahead_send.at[2 * AHEAD], recv_sem=ahead_recv.at[2 * AHEAD],
         device_id=(r, at_chip(1)), device_id_type=MESH,
     )
     mask_pass = pltpu.make_async_remote_copy(
-        src_ref=mask_ahead.at[core], dst_ref=mask_ahead.at[core], send_sem=pass_send.at[AHEAD],
-        recv_sem=pass_recv.at[AHEAD], device_id=(r, partner), device_id_type=MESH,
+        src_ref=mask_ahead.at[core], dst_ref=mask_ahead.at[core], send_sem=pass_send.at[2 * AHEAD],
+        recv_sem=pass_recv.at[2 * AHEAD], device_id=(r, partner), device_id_type=MESH,
     )
     mask_copy.start()
-    ahead_copy(0).start()
+    for n in range(EARLY):
+        ahead_copy(n).start()
 
     def wait_pieces(d, carry):
         for copy in piece_copies(d):
@@ -181,11 +186,11 @@
                 )
         return out
 
-    back_one = halves(0, 2, 0, -1, 0)
+    back_one = (halves(0, 1, 0, -1, 0), halves(1, 1, 1, -1, 3))
     stay = halves(0, 3, 2, 0, 1)[2:]
     stay_odd = halves(3, 1, 5, 0, 2)[2:]
     back_two = halves(3, 1, 5, -2, 2)
-    for copy in back_one:
+    for copy in back_one[0] + back_one[1]:
         copy.start()
 
     @pl.when(core == 0)
@@ -202,15 +207,15 @@
             copy.start()
 
     turn = 1 - 2 * core
-    hops = [(0, 1), (0, -1)]
     if depth_z > 4:
-        hops += [(0, 2), (0, -2), (2, 1), (-2, -1), (2 * turn, 2 * turn)]
+        hops = [(0, 2), (0, -2), (0, 1), (0, -1), (2, 1), (-2, -1), (2 * turn, 2 * turn)]
     else:
-        hops += [(0, 2 * turn)]
+        hops = [(0, 2 * turn), (0, 1), (0, -1)]
     direct = 4 if depth_z > 4 else 3
 
     def strips_of(which, back):
-        return (p_a, p_t, p_l, p_c)[which].at[lax.rem(z - back + depth_z, depth_z)]
+        buf, slot = ((p_a, 0), (p_a, 1), (p_t, 0), (p_l, 0), (p_c, 0), (p_c, 1))[which]
+        return buf.at[lax.rem(z - back + depth_z, depth_z), slot]
 
     def hop_copy(which, n):
         behind, on = hops[n]
@@ -234,22 +239,22 @@
 
     def ring_second(which):
         if direct < len(hops):
-            hop_received(which, 2)
-            hop_received(which, 3)
+            hop_received(which, 0)
+            hop_received(which, 1)
         for n in range(direct, len(hops)):
             hop_copy(which, n).start()
 
     def ring_rest(which):
         for n in range(len(hops)):
-            if direct == len(hops) or n not in (2, 3):
+            if direct == len(hops) or n not in (0, 1):
                 hop_received(which, n)
 
     def ring_drain(which):
         for n in range(len(hops)):
             hop_copy(which, n).wait_send()
 
-    def assemble(fac, strips, weights):
-        for slot in range(weights.shape[0]):
+    def assemble(fac, strips, weights, *slots):
+        for slot in slots:
             factors = []
             for k in range(2):
                 for t in range(tiles):
@@ -285,7 +290,7 @@
                 recv_sem=one_recv.at[0, i], device_id=where, device_id_type=MESH,
             ),
             pltpu.make_async_remote_copy(
-                src_ref=s_scale.at[i], dst_ref=r_one_scale.at[i], send_sem=one_send.at[1, i],
+                src_ref=s_scale.at[i, pl.ds(0, 1)], dst_ref=r_one_scale.at[i, pl.ds(0, 1)], send_sem=one_send.at[1, i],
                 recv_sem=one_recv.at[1, i], device_id=where, device_id_type=MESH,
             ),
         )
@@ -298,17 +303,18 @@
                 recv_sem=two_recv.at[0, i], device_id=where, device_id_type=MESH,
             ),
             pltpu.make_async_remote_copy(
-                src_ref=t_scale.at[i], dst_ref=r_two_scale.at[i], send_sem=two_send.at[1, i],
+                src_ref=t_scale.at[i, pl.ds(0, 1)], dst_ref=r_two_scale.at[i, pl.ds(0, 1)], send_sem=two_send.at[1, i],
                 recv_sem=two_recv.at[1, i], device_id=where, device_id_type=MESH,
             ),
         )
 
-    for copy in back_one:
-        copy.wait_recv()
     for slot in (0, 1):
+        for copy in back_one[slot]:
+            copy.wait_recv()
         p_a[z, slot] = got_s[0, slot] + got_s[1, slot]
         fac_a[slot] = got_f[0, slot] + got_f[1, slot]
-    ring_first(0)
+        ring_first(slot)
+    ring_second(0)
 
     @pl.when(core == 0)
     def _():
@@ -326,17 +332,19 @@
 
     for copy in stay:
         copy.wait_recv()
-    for i in range(1, AHEAD):
-        ahead_copy(i).start()
+    for n in range(EARLY, 2 * AHEAD):
+        ahead_copy(n).start()
     p_l[z, 0] = half_s[2] + got_s[1, 4]
     fac_l[0] = half_f[2] + got_f[1, 4]
     for slot in (0, 1):
         p_c[z, slot] = half_s[slot] + got_s[1, 2 + slot]
         fac_c[slot] = half_f[slot] + got_f[1, 2 + slot]
-    ring_second(0)
-    ring_first(1)
+    ring_second(1)
     ring_rest(0)
-    assemble(fac_a, p_a, w_a)
+    assemble(fac_a, p_a, w_a, 0)
+    ring_first(2)
+    ring_rest(1)
+    assemble(fac_a, p_a, w_a, 1)
     own_amp.wait()
     for copy in swaps:
         copy.wait_recv()
@@ -346,17 +354,17 @@
         x = x + jnp.dot(masked(1, i), w_a[1], preferred_element_type=F32)
         code, scale = coded(x)
         s_out[rows(i)] = code
-        s_scale[i] = jnp.broadcast_to(scale, (8, tile))
+        s_scale[i, 0:1] = scale
         for copy in flow_one(i):
             copy.start()
 
     def received(buf, scale, i):
-        return buf[rows(i)].astype(jnp.int32).astype(F32) * scale[i][0:1]
+        return buf[rows(i)].astype(jnp.int32).astype(F32) * scale[i, 0:1]
 
     def send_two(i, x):
         code, scale = coded(x)
         t_out[rows(i)] = code
-        t_scale[i] = jnp.broadcast_to(scale, (8, tile))
+        t_scale[i, 0:1] = scale
         for copy in flow_two(i):
             copy.start()
 
@@ -418,36 +426,38 @@
     late = blocks - AHEAD
     cuts = [AHEAD + late * k // 4 for k in range(5)]
     each(cuts[0], cuts[1], outward)
-    ring_second(1)
-    for which in (2, 3):
+    ring_second(2)
+    for which in (3, 4, 5):
         ring_first(which)
     each(cuts[1], cuts[2], outward)
-    ring_rest(1)
-    assemble(fac_t, p_t, w_t)
+    ring_rest(2)
+    assemble(fac_t, p_t, w_t, 0)
     each(0, AHEAD, lambda i: odd_term(i, True))
     each(cuts[0], cuts[1], lambda i: odd_term(i, False))
     each(cuts[2], cuts[3], outward)
-    for which in (2, 3):
+    for which in (3, 4, 5):
         ring_second(which)
     each(cuts[1], cuts[2], lambda i: odd_term(i, False))
     each(cuts[3], cuts[4], outward)
     mask_copy.wait_recv()
     mask_pass.start()
-    for i in range(AHEAD):
-        ahead_copy(i).wait_recv()
-        pass_copy(i).start()
+    for n in range(2 * AHEAD):
+        ahead_copy(n).wait_recv()
+        pass_copy(n).start()
     each(cuts[2], cuts[4], lambda i: odd_term(i, False))
     each(cuts[0], cuts[1], relay)
-    ring_rest(2)
-    assemble(fac_l, p_l, w_l)
+    ring_rest(3)
+    assemble(fac_l, p_l, w_l, 0)
     each(0, blocks, here)
     each(cuts[1], cuts[2], relay)
-    ring_rest(3)
-    assemble(fac_c, p_c, w_c)
+    ring_rest(4)
+    ring_rest(5)
+    assemble(fac_c, p_c, w_c, 0, 1)
     mask_pass.wait_recv()
 
     def from_ahead(i):
-        pass_copy(i).wait_recv()
+        pass_copy(2 * i).wait_recv()
+        pass_copy(2 * i + 1).wait_recv()
         local[rows(i)] = (
             local[rows(i)]
             + jnp.dot(masked(0, i, mask_ahead, ahead), w_c[0], preferred_element_type=F32)
@@ -468,7 +478,7 @@
         return carry
 
     lax.fori_loop(1, depth_z, drain_pieces, 0)
-    for copy in list(swaps) + back_one + stay:
+    for copy in list(swaps) + back_one[0] + back_one[1] + stay:
         copy.wait_send()
 
     @pl.when(core == 0)
@@ -481,13 +491,13 @@
         for copy in stay_odd:
             copy.wait_send()
 
-    for which in (0, 1, 2, 3):
+    for which in range(6):
         ring_drain(which)
     for copy in (mask_copy, mask_pass):
         copy.wait_send()
-    for i in range(AHEAD):
-        ahead_copy(i).wait_send()
-        pass_copy(i).wait_send()
+    for n in range(2 * AHEAD):
+        ahead_copy(n).wait_send()
+        pass_copy(n).wait_send()
 
     def drain_one(i, carry):
         for copy in flow_one(i):
@@ -558,10 +568,10 @@
             code, scale, code, scale, code, scale, code, scale,
             vmem((count, tile), BF16),
             dma((2,)), dma((2,)), dma((2,)),
-            dma((AHEAD + 1,)), dma((AHEAD + 1,)), dma((AHEAD + 1,)), dma((AHEAD + 1,)),
+            dma((2 * AHEAD + 1,)), dma((2 * AHEAD + 1,)), dma((2 * AHEAD + 1,)), dma((2 * AHEAD + 1,)),
             dma((2, depth_z)), dma((2, depth_z)),
-            dma((3, 2, 2)), dma((3, 2, 2)),
-            dma((4, hops)), dma((4, hops)),
+            dma((4, 2, 2)), dma((4, 2, 2)),
+            dma((6, hops)), dma((6, hops)),
             dma((2, blocks)), dma((2, blocks)),
             dma((2, blocks)), dma((2, blocks)),
             dma((blocks,)),

time: 82.5 us -> 80.9 us (0.981)
  Pallas kernels: 75.3 us -> 74.1 us
    pallas_call x1, Pallas kernels: 75.3 us -> 74.1 us  [shards(): pl.pallas_call(functools.partial(kernel, rows_of, cols_of), out_shape=jax...]
where the time goes in v3:
time: 80.9 us; the launch traced here: 80.1 us
  Pallas kernels  74.1 us (92%)
  local copies, waits for them, and re-layouts  5.32 us (7%)
    pallas_call x1, Pallas kernels, shards(): pl.pallas_call(functools.partial(kernel, rows_of, cols_of), out_shape=jax...  74.1 us
    unnamed x3, local copies, waits for them, and re-layouts  5.32 us

profile of v3, /device:TPU:2, one launch (start us, length us, event | category | flops | bytes accessed | tf_op | source)
XLA Modules:
  0.0 80.1 jit_solution(11161955965089013846)
XLA Ops:
  0.7 1.3 %copy.7.owner_ref = s32[4,1]{1,0:T(4,128)} copy(s32[4,1]{0,1:T(1,128)} %param.11) | data formatting | bytes 32 | tf_op args[5]
  2.0 1.4 %copy.8.mask_ref = s32[12,3]{1,0:T(8,128)} copy(s32[12,3]{0,1:T(4,128)} %param.7) | data formatting | bytes 288 | tf_op args[1]
  3.3 74.1 %shard_map.64 = bf16[3072,256]{1,0:T(8,128)(2,1)} custom-call(s32[4,1]{1,0:T(4,128)} %copy.7.owner_ref, s32[1,1,2]{2,1,0:T(1,128)} %list_ref.1, s32[1,1]{1,0:T(1,128)S(6)} %copy.10.count_ref, s32[12,3]{1,0:T(8,128)} %copy.8.mask_ref, bf16[3072,768]{1,0:T(8,128)(2,1)} %amp.1, bf16[2,256,256]{2,1,0:T(8,128)(2,1)} %bitcast.1), custom_call_target="tpu_custom_call" | custom-call | tf_op jit(solution)/shard_map/pallas_call | solution.py:540
  77.5 2.7 %copy.11 = bf16[3072,256]{1,0:T(8,128)(2,1)} copy(bf16[3072,256]{1,0:T(8,128)(2,1)} %shard_map.64) | data formatting | bytes 3145728

commit v4 on v3

--- a/solution.py
+++ b/solution.py
@@ -21,9 +21,9 @@
 def kernel(
     rows_of, cols_of, owner_ref, list_ref, count_ref, mask_ref, amp, panel, out,
     both, maskv, ahead, mask_ahead, meta, meta_in, piece_in, half_s, half_f, got_s, got_f, fac_a, fac_t, fac_l, fac_c,
-    p_a, p_t, p_l, p_c, w_a, w_t, w_l, w_c, local, t_own, s_out, s_scale, r_one, r_one_scale, t_out, t_scale, r_two, r_two_scale, result,
+    p_a, p_t, p_l, p_c, w_a, w_t, w_l, w_c, local, t_own, s_out, s_scale, r_one, r_one_scale, t_out, t_scale, r_two, r_two_scale, leg, leg_scale, result,
     amp_sem, amp_send, amp_recv, ahead_send, ahead_recv, pass_send, pass_recv,
-    a2a_send, a2a_recv, shift_send, shift_recv, ring_send, ring_recv, one_send, one_recv, two_send, two_recv, out_sem,
+    a2a_send, a2a_recv, shift_send, shift_recv, ring_send, ring_recv, one_send, one_recv, two_send, two_recv, leg_send, leg_recv, out_sem,
 ):
     r, c = lax.axis_index("row"), lax.axis_index("col")
     depth_z = rows_of // 2
@@ -40,11 +40,11 @@
     def at_chip(step, same_core=True):
         return lax.rem(chip + step + chips, chips) * 2 + core
 
-    row_id = lax.broadcasted_iota(jnp.int32, (8, 128), 0)
+    lane = lax.broadcasted_iota(jnp.int32, (8, 128), 1)
     flags = jnp.zeros((8, 128), F32)
     for k in range(2):
         live = jnp.where(k < count_ref[0, 0], k * tiles + list_ref[0, 0, k], -1)
-        flags = flags + jnp.where(row_id == live, 1.0, 0.0)
+        flags = flags + jnp.where(lane == live, 1.0, 0.0)
     meta[...] = flags
     meta_in[z] = flags
     for t in range(tiles):
@@ -91,8 +91,8 @@
                 device_id_type=MESH,
             ),
             pltpu.make_async_remote_copy(
-                src_ref=meta,
-                dst_ref=meta_in.at[z],
+                src_ref=meta.at[pl.ds(0, 1)],
+                dst_ref=meta_in.at[z, pl.ds(0, 1)],
                 send_sem=a2a_send.at[1, d],
                 recv_sem=a2a_recv.at[1, d],
                 device_id=(y * depth_z + peer, c),
@@ -161,17 +161,17 @@
     def chosen(even_step, odd_step):
         holder = owner_ref[pl.ds(even_step * (1 - core) + odd_step * core, 1), :] - y * depth_z
         wide = jnp.broadcast_to(holder, (strip, tile))
-        small = jnp.broadcast_to(holder, (8, 128))
-        first, second, factors = jnp.zeros((strip, tile), BF16), jnp.zeros((strip, tile), BF16), jnp.zeros((8, 128), F32)
+        small = jnp.broadcast_to(holder, (1, 128))
+        first, second, factors = jnp.zeros((strip, tile), BF16), jnp.zeros((strip, tile), BF16), jnp.zeros((1, 128), F32)
         for j in range(depth_z):
             named = jnp.where(wide == j, 1.0, 0.0).astype(BF16)
             first = first + named * piece_in[j, 0]
             second = second + named * piece_in[j, 1]
-            factors = factors + jnp.where(small == j, meta_in[j], 0.0)
+            factors = factors + jnp.where(small == j, meta_in[j, 0:1], 0.0)
         return first, second, factors
 
     for slot, steps in enumerate(((2, 3), (1, 2), (0, 1), (3, 0))):
-        half_s[slot, 0], half_s[slot, 1], half_f[slot] = chosen(*steps)
+        half_s[slot, 0], half_s[slot, 1], half_f[slot, 0:1] = chosen(*steps)
 
     def halves(first, count, landing, step, n):
         out = []
@@ -179,7 +179,8 @@
             for k, (src, dst) in enumerate(((half_s, got_s), (half_f, got_f))):
                 out.append(
                     pltpu.make_async_remote_copy(
-                        src_ref=src.at[pl.ds(first, count)], dst_ref=dst.at[m, pl.ds(landing, count)],
+                        src_ref=src.at[(pl.ds(first, count), pl.ds(0, 1))[: 1 + k]],
+                        dst_ref=dst.at[(m, pl.ds(landing, count), pl.ds(0, 1))[: 2 + k]],
                         send_sem=shift_send.at[n, m, k], recv_sem=shift_recv.at[n, m, k],
                         device_id=(row, at_chip(step)), device_id_type=MESH,
                     )
@@ -258,8 +259,8 @@
             factors = []
             for k in range(2):
                 for t in range(tiles):
-                    f = jnp.broadcast_to(fac[slot, k * tiles + t : k * tiles + t + 1, :], (strip, 128))
-                    factors.append(jnp.concatenate([f] * (tile // 128), axis=1).astype(BF16))
+                    f = fac[slot, 0:1, k * tiles + t : k * tiles + t + 1]
+                    factors.append(jnp.broadcast_to(f, (strip, tile)).astype(BF16))
 
             def put(i, carry):
                 first, second = strips[i, slot, 0], strips[i, slot, 1]
@@ -282,6 +283,38 @@
 
     one_chip = 1 - 2 * y_lo * (1 - core)
 
+    def by_x(i):
+        return (core == 1) & (y_lo == 1) & (lax.rem(i, 2) == 1)
+
+    def first_leg(i):
+        return [
+            pltpu.make_async_remote_copy(
+                src_ref=src, dst_ref=dst, send_sem=leg_send.at[k, i], recv_sem=leg_recv.at[k, i],
+                device_id=(r, at_chip(2)), device_id_type=MESH,
+            )
+            for k, (src, dst) in enumerate(
+                ((s_out.at[rows(i)], leg.at[rows(i)]), (s_scale.at[i, pl.ds(0, 1)], leg_scale.at[i, pl.ds(0, 1)]))
+            )
+        ]
+
+    def second_leg(i):
+        return [
+            pltpu.make_async_remote_copy(
+                src_ref=src, dst_ref=dst, send_sem=one_send.at[k, i], recv_sem=one_recv.at[k, i],
+                device_id=(r, at_chip(-1)), device_id_type=MESH,
+            )
+            for k, (src, dst) in enumerate(
+                ((leg.at[rows(i)], r_one.at[rows(i)]), (leg_scale.at[i, pl.ds(0, 1)], r_one_scale.at[i, pl.ds(0, 1)]))
+            )
+        ]
+
+    def pass_on(i):
+        @pl.when(by_x(i))
+        def _():
+            for first, second in zip(first_leg(i), second_leg(i)):
+                first.wait_recv()
+                second.start()
+
     def flow_one(i):
         where = (r, at_chip(one_chip))
         return (
@@ -312,7 +345,7 @@
         for copy in back_one[slot]:
             copy.wait_recv()
         p_a[z, slot] = got_s[0, slot] + got_s[1, slot]
-        fac_a[slot] = got_f[0, slot] + got_f[1, slot]
+        fac_a[slot, 0:1] = got_f[0, slot, 0:1] + got_f[1, slot, 0:1]
         ring_first(slot)
     ring_second(0)
 
@@ -321,24 +354,24 @@
         for copy in back_two:
             copy.wait_recv()
         p_t[z, 0] = got_s[0, 5] + got_s[1, 5]
-        fac_t[0] = got_f[0, 5] + got_f[1, 5]
+        fac_t[0, 0:1] = got_f[0, 5, 0:1] + got_f[1, 5, 0:1]
 
     @pl.when(core == 1)
     def _():
         for copy in stay_odd:
             copy.wait_recv()
         p_t[z, 0] = half_s[3] + got_s[1, 5]
-        fac_t[0] = half_f[3] + got_f[1, 5]
+        fac_t[0, 0:1] = half_f[3, 0:1] + got_f[1, 5, 0:1]
 
     for copy in stay:
         copy.wait_recv()
     for n in range(EARLY, 2 * AHEAD):
         ahead_copy(n).start()
     p_l[z, 0] = half_s[2] + got_s[1, 4]
-    fac_l[0] = half_f[2] + got_f[1, 4]
+    fac_l[0, 0:1] = half_f[2, 0:1] + got_f[1, 4, 0:1]
     for slot in (0, 1):
         p_c[z, slot] = half_s[slot] + got_s[1, 2 + slot]
-        fac_c[slot] = half_f[slot] + got_f[1, 2 + slot]
+        fac_c[slot, 0:1] = half_f[slot, 0:1] + got_f[1, 2 + slot, 0:1]
     ring_second(1)
     ring_rest(0)
     assemble(fac_a, p_a, w_a, 0)
@@ -355,8 +388,15 @@
         code, scale = coded(x)
         s_out[rows(i)] = code
         s_scale[i, 0:1] = scale
-        for copy in flow_one(i):
-            copy.start()
+        @pl.when(by_x(i))
+        def _():
+            for copy in first_leg(i):
+                copy.start()
+
+        @pl.when(jnp.logical_not(by_x(i)))
+        def _():
+            for copy in flow_one(i):
+                copy.start()
 
     def received(buf, scale, i):
         return buf[rows(i)].astype(jnp.int32).astype(F32) * scale[i, 0:1]
@@ -425,20 +465,32 @@
 
     late = blocks - AHEAD
     cuts = [AHEAD + late * k // 4 for k in range(5)]
-    each(cuts[0], cuts[1], outward)
+    @pl.when(core == 0)
+    def _():
+        each(cuts[0], cuts[1], outward)
+
     ring_second(2)
     for which in (3, 4, 5):
         ring_first(which)
-    each(cuts[1], cuts[2], outward)
+    @pl.when(core == 0)
+    def _():
+        each(cuts[1], cuts[2], outward)
+
+    @pl.when(core == 1)
+    def _():
+        each(cuts[0], cuts[2], outward)
+
     ring_rest(2)
     assemble(fac_t, p_t, w_t, 0)
     each(0, AHEAD, lambda i: odd_term(i, True))
     each(cuts[0], cuts[1], lambda i: odd_term(i, False))
+    each(cuts[0], cuts[1], pass_on)
     each(cuts[2], cuts[3], outward)
     for which in (3, 4, 5):
         ring_second(which)
     each(cuts[1], cuts[2], lambda i: odd_term(i, False))
     each(cuts[3], cuts[4], outward)
+    each(cuts[1], cuts[2], pass_on)
     mask_copy.wait_recv()
     mask_pass.start()
     for n in range(2 * AHEAD):
@@ -465,10 +517,12 @@
         )
         finish(i, True)
 
+    each(cuts[2], cuts[3], pass_on)
     each(0, AHEAD, from_ahead)
     ready = cuts[2] - LAG
     assert ready >= AHEAD
     each(AHEAD, ready, lambda i: finish(i, False))
+    each(cuts[3], cuts[4], pass_on)
     each(cuts[2], blocks, relay, lambda i: finish(i - LAG, False))
     each(blocks - LAG, blocks, lambda i: finish(i, False))
 
@@ -500,6 +554,11 @@
         pass_copy(n).wait_send()
 
     def drain_one(i, carry):
+        @pl.when(by_x(i))
+        def _():
+            for copy in first_leg(i):
+                copy.wait_send()
+
         for copy in flow_one(i):
             copy.wait_send()
         return carry
@@ -565,13 +624,14 @@
             vmem((2, width, tile), BF16),
             vmem((count, tile), F32),
             vmem((count, tile), F32),
-            code, scale, code, scale, code, scale, code, scale,
+            code, scale, code, scale, code, scale, code, scale, code, scale,
             vmem((count, tile), BF16),
             dma((2,)), dma((2,)), dma((2,)),
             dma((2 * AHEAD + 1,)), dma((2 * AHEAD + 1,)), dma((2 * AHEAD + 1,)), dma((2 * AHEAD + 1,)),
             dma((2, depth_z)), dma((2, depth_z)),
             dma((4, 2, 2)), dma((4, 2, 2)),
             dma((6, hops)), dma((6, hops)),
+            dma((2, blocks)), dma((2, blocks)),
             dma((2, blocks)), dma((2, blocks)),
             dma((2, blocks)), dma((2, blocks)),
             dma((blocks,)),

time: 80.9 us -> 80 us (0.989)
  no operation moved by 1% of the time
where the time goes in v4:
time: 80 us; the launch traced here: 79.8 us
  Pallas kernels  73.8 us (92%)
  local copies, waits for them, and re-layouts  5.32 us (7%)
    pallas_call x1, Pallas kernels, shards(): pl.pallas_call(functools.partial(kernel, rows_of, cols_of), out_shape=jax...  73.8 us
    unnamed x3, local copies, waits for them, and re-layouts  5.32 us

profile of v4, /device:TPU:2, one launch (start us, length us, event | category | flops | bytes accessed | tf_op | source)
XLA Modules:
  0.0 79.8 jit_solution(6733635307835535734)
XLA Ops:
  0.7 1.3 %copy.7.owner_ref = s32[4,1]{1,0:T(4,128)} copy(s32[4,1]{0,1:T(1,128)} %param.11) | data formatting | bytes 32 | tf_op args[5]
  2.0 1.4 %copy.8.mask_ref = s32[12,3]{1,0:T(8,128)} copy(s32[12,3]{0,1:T(4,128)} %param.7) | data formatting | bytes 288 | tf_op args[1]
  3.3 73.8 %shard_map.64 = bf16[3072,256]{1,0:T(8,128)(2,1)} custom-call(s32[4,1]{1,0:T(4,128)} %copy.7.owner_ref, s32[1,1,2]{2,1,0:T(1,128)} %list_ref.1, s32[1,1]{1,0:T(1,128)S(6)} %copy.10.count_ref, s32[12,3]{1,0:T(8,128)} %copy.8.mask_ref, bf16[3072,768]{1,0:T(8,128)(2,1)} %amp.1, bf16[2,256,256]{2,1,0:T(8,128)(2,1)} %bitcast.1), custom_call_target="tpu_custom_call" | custom-call | tf_op jit(solution)/shard_map/pallas_call | solution.py:599
  77.1 2.7 %copy.11 = bf16[3072,256]{1,0:T(8,128)(2,1)} copy(bf16[3072,256]{1,0:T(8,128)(2,1)} %shard_map.64) | data formatting | bytes 3145728
